TPU v7x, 32 devices: a whole 2x2x4 slice. The times are simulated.
32 devices in a mesh: dp: 8 (over z, y), row: 2 (over core), col: 2 (over x).
Axes of the slice: x: 2, y: 2, z: 4, core: 2. Of those that a mesh axis runs over, the one named last changes fastest.
Arguments:
- tokens: bfloat16 [32768, 1024], P('dp', ('row', 'col')), may hold values from -6 to 6
- first_gain: float32 [1024], P(('row', 'col')), may hold values from 0.5 to 1.5
- first_shift: float32 [1024], P(('row', 'col')), may hold values from -3 to 3
- joined_weight: bfloat16 [1024, 3072], P('row', 'col'), may hold values from -0.1875 to 0.1875
- query_value_bias: float32 [16, 128], P(('col', 'row')), may hold values from -3 to 3
- output_weight: bfloat16 [1024, 1024], P('col', 'row'), may hold values from -0.375 to 0.375
- output_bias: float32 [1024], P(('row', 'col')), may hold values from -3 to 3
- second_gain: float32 [1024], P(('row', 'col')), may hold values from 0.5 to 1.5
- second_shift: float32 [1024], P(('row', 'col')), may hold values from -3 to 3
- up_weight: bfloat16 [1024, 4096], P('row', 'col'), may hold values from -0.1875 to 0.1875
- up_bias: float32 [4096], P(('col', 'row')), may hold values from -3 to 3
- down_weight: bfloat16 [4096, 1024], P('col', 'row'), may hold values from -0.09375 to 0.09375
- down_bias: float32 [1024], P(('row', 'col')), may hold values from -3 to 3
- out_grad: bfloat16 [32768, 1024], P('dp', ('row', 'col')), may hold values from -6 to 6
Outputs:
- result: bfloat16 [32768, 1024], P('dp', ('row', 'col'))
- tokens_grad: float32 [32768, 1024], P('dp', ('row', 'col'))
- first_gain_grad: float32 [1024], P(('row', 'col'))
- first_shift_grad: float32 [1024], P(('row', 'col'))
- joined_weight_grad: float32 [1024, 3072], P('row', 'col')
- query_value_bias_grad: float32 [16, 128], P(('col', 'row'))
- output_weight_grad: float32 [1024, 1024], P('col', 'row')
- output_bias_grad: float32 [1024], P(('row', 'col'))
- second_gain_grad: float32 [1024], P(('row', 'col'))
- second_shift_grad: float32 [1024], P(('row', 'col'))
- up_weight_grad: float32 [1024, 4096], P('row', 'col')
- up_bias_grad: float32 [4096], P(('col', 'row'))
- down_weight_grad: float32 [4096, 1024], P('col', 'row')
- down_bias_grad: float32 [1024], P(('row', 'col'))
All inputs are finite; a program needn't handle non-finite values.
Results may differ from a plain program's by a relative error of at most 0.009.
Values may be sent and summed in bfloat16 or wider, within the bound.
A program may use at most 320 MiB of HBM per device.

v0:
```python
from functools import partial

import jax
import jax.numpy as jnp
from jax import lax
from jax.sharding import PartitionSpec as P

D = 1024
H = 16
HD = 64
SEQ_LEN = 1024
QB = 512


EPSILON = 1e-05


def stats_total(first, second):
    return lax.psum((first, second), ("row", "col"))


def column_gather(values):
    return lax.all_gather(values, "col", axis=1, tiled=True)


def column_total(partial_sums):
    return lax.psum_scatter(partial_sums, "col", scatter_dimension=1, tiled=True)


def row_gather(values):
    return lax.all_gather(values, "row", axis=1, tiled=True)


def row_total(partial_sums):
    return lax.psum_scatter(partial_sums, "row", scatter_dimension=1, tiled=True)


def settle_upper(first, second, third, fourth, fifth, sixth):
    return (first, second, third, fourth, fifth, sixth)


def norm_forward(inputs, norm_gain, norm_shift, totals):
    row_sum, square_sum = totals(jnp.sum(inputs, axis=1), jnp.sum(inputs * inputs, axis=1))
    average = row_sum / D
    variance = square_sum / D - average * average
    scale_rows = lax.rsqrt(variance + EPSILON)
    centered = (inputs - average[:, None]) * scale_rows[:, None]
    return (centered, scale_rows, (centered * norm_gain + norm_shift).astype(jnp.bfloat16))


def norm_backward(upstream, centered, scale_rows, norm_gain, totals):
    scaled = upstream * norm_gain
    row_sum, mixed_sum = totals(jnp.sum(scaled, axis=1), jnp.sum(scaled * centered, axis=1))
    inputs_grad = scale_rows[:, None] * (
        scaled - row_sum[:, None] / D - centered * (mixed_sum[:, None] / D)
    )
    return (inputs_grad, jnp.sum(upstream * centered, axis=0), jnp.sum(upstream, axis=0))


def slopes_from(first_head, head_count):
    head_ids = (first_head + jnp.arange(head_count)).astype(jnp.float32)
    return jnp.exp2(-8.0 * (head_ids + 1.0) / H)


def joined_bias(query_value_bias, head_count):
    pair_bias = query_value_bias.reshape(head_count, 2, HD)
    zero_block = jnp.zeros((head_count, 1, HD), jnp.float32)
    return jnp.concatenate([pair_bias[:, :1], zero_block, pair_bias[:, 1:]], axis=1).reshape(-1)


def block_scores(query_rows, key_rows, slopes, block_start):
    raw_scores = jnp.einsum(
        "sqhd,skhd->shqk", query_rows, key_rows, preferred_element_type=jnp.float32
    )
    query_pos = block_start + jnp.arange(query_rows.shape[1])
    key_pos = jnp.arange(key_rows.shape[1])
    distance = (query_pos[:, None] - key_pos[None, :]).astype(jnp.float32)
    scores = raw_scores * HD ** (-0.5) - slopes[:, None, None] * distance
    return jnp.where(distance >= 0, scores, -1e30)


def attend(joined_rows, slopes):
    queries = joined_rows[:, :, :, 0]
    key_rows = joined_rows[:, :, :, 1]
    value_rows = joined_rows[:, :, :, 2]
    pieces = []
    log_sums = []
    for block_start in range(0, SEQ_LEN, QB):
        block_stop = block_start + QB
        scores = block_scores(
            queries[:, block_start:block_stop], key_rows[:, :block_stop], slopes, block_start
        )
        row_max = jnp.max(scores, axis=-1, keepdims=True)
        exponentials = jnp.exp(scores - row_max)
        row_total_sum = jnp.sum(exponentials, axis=-1, keepdims=True)
        soft_weights = (exponentials / row_total_sum).astype(jnp.bfloat16)
        pieces.append(
            jnp.einsum(
                "shqk,skhd->sqhd",
                soft_weights,
                value_rows[:, :block_stop],
                preferred_element_type=jnp.float32,
            )
        )
        log_sums.append(row_max + jnp.log(row_total_sum))
    return (jnp.concatenate(pieces, axis=1).astype(jnp.bfloat16), jnp.concatenate(log_sums, axis=2))


def attend_back(joined_rows, slopes, log_sums, out_grads):
    scale = HD ** (-0.5)
    queries = joined_rows[:, :, :, 0]
    key_rows = joined_rows[:, :, :, 1]
    value_rows = joined_rows[:, :, :, 2]
    query_grads = []
    key_grads = jnp.zeros(key_rows.shape, jnp.float32)
    value_grads = jnp.zeros(value_rows.shape, jnp.float32)
    for block_start in range(0, SEQ_LEN, QB):
        block_stop = block_start + QB
        key_block = key_rows[:, :block_stop]
        value_block = value_rows[:, :block_stop]
        query_block = queries[:, block_start:block_stop]
        out_block = out_grads[:, block_start:block_stop]
        scores = block_scores(query_block, key_block, slopes, block_start)
        chances = jnp.exp(scores - log_sums[:, :, block_start:block_stop])
        prob_grads = jnp.einsum(
            "sqhd,skhd->shqk", out_block, value_block, preferred_element_type=jnp.float32
        )
        score_grads = (
            chances * (prob_grads - jnp.sum(chances * prob_grads, axis=-1, keepdims=True))
        ).astype(jnp.bfloat16)
        query_grads.append(
            jnp.einsum(
                "shqk,skhd->sqhd", score_grads, key_block, preferred_element_type=jnp.float32
            )
            * scale
        )
        key_grads = key_grads.at[:, :block_stop].add(
            jnp.einsum(
                "shqk,sqhd->skhd", score_grads, query_block, preferred_element_type=jnp.float32
            )
            * scale
        )
        value_grads = value_grads.at[:, :block_stop].add(
            jnp.einsum(
                "shqk,sqhd->skhd",
                chances.astype(jnp.bfloat16),
                out_block,
                preferred_element_type=jnp.float32,
            )
        )
    return jnp.stack([jnp.concatenate(query_grads, axis=1), key_grads, value_grads], axis=3).astype(
        jnp.bfloat16
    )


def blocks_layer(
    tokens,
    first_gain,
    first_shift,
    joined_weight,
    query_value_bias,
    output_weight,
    output_bias,
    second_gain,
    second_shift,
    up_weight,
    up_bias,
    down_weight,
    down_bias,
    out_grad,
):
    row_count = tokens.shape[0]
    seq_count = row_count // SEQ_LEN
    head_count = query_value_bias.shape[0]
    inputs = tokens.astype(jnp.float32)
    centered_first, scale_first, normed_first = norm_forward(
        inputs, first_gain, first_shift, stats_total
    )
    wide_first = column_gather(normed_first)
    joined_part = jnp.dot(wide_first, joined_weight, preferred_element_type=jnp.float32)
    joined_flat = row_total(joined_part)
    joined_rows = (
        (joined_flat + joined_bias(query_value_bias, head_count))
        .astype(jnp.bfloat16)
        .reshape(seq_count, SEQ_LEN, head_count, 3, HD)
    )
    block_index = lax.axis_index("col") * lax.axis_size("row") + lax.axis_index("row")
    slopes = slopes_from(block_index * head_count, head_count)
    attended, log_sums = attend(joined_rows, slopes)
    attended = attended.reshape(row_count, head_count * HD)
    mixed_heads = row_gather(attended)
    hidden = (
        inputs
        + column_total(jnp.dot(mixed_heads, output_weight, preferred_element_type=jnp.float32))
        + output_bias
    )
    centered_second, scale_second, normed_second = norm_forward(
        hidden, second_gain, second_shift, stats_total
    )
    wide_second = column_gather(normed_second)
    up_part = jnp.dot(wide_second, up_weight, preferred_element_type=jnp.float32)
    preact = row_total(up_part) + up_bias
    activated = jax.nn.gelu(preact, approximate=True).astype(jnp.bfloat16)
    act_wide = row_gather(activated)
    outcome = (
        hidden
        + column_total(jnp.dot(act_wide, down_weight, preferred_element_type=jnp.float32))
        + down_bias
    )
    upstream = out_grad.astype(jnp.float32)
    down_bias_grad = jnp.sum(upstream, axis=0)
    grad_wide = column_gather(out_grad)
    down_weight_grad = jnp.einsum(
        "tf,td->fd", act_wide, grad_wide, preferred_element_type=jnp.float32
    )
    act_part = jnp.einsum("td,fd->tf", grad_wide, down_weight, preferred_element_type=jnp.float32)
    activated_grad = row_total(act_part)
    gelu_value, gelu_pull = jax.vjp(partial(jax.nn.gelu, approximate=True), preact)
    preact_grad = gelu_pull(activated_grad)[0].astype(jnp.bfloat16)
    up_bias_grad = jnp.sum(preact_grad.astype(jnp.float32), axis=0)
    preact_wide = row_gather(preact_grad)
    up_weight_grad = jnp.einsum(
        "td,tf->df", wide_second, preact_wide, preferred_element_type=jnp.float32
    )
    normed_second_grad = column_total(
        jnp.einsum("tf,df->td", preact_wide, up_weight, preferred_element_type=jnp.float32)
    )
    back_second, second_gain_grad, second_shift_grad = norm_backward(
        normed_second_grad, centered_second, scale_second, second_gain, stats_total
    )
    upper = settle_upper(
        down_weight_grad,
        down_bias_grad,
        up_weight_grad,
        up_bias_grad,
        second_gain_grad,
        second_shift_grad,
    )
    hidden_grad = upstream + back_second
    output_bias_grad = jnp.sum(hidden_grad, axis=0)
    branch_wide = column_gather(hidden_grad.astype(jnp.bfloat16))
    output_weight_grad = jnp.einsum(
        "th,td->hd", mixed_heads, branch_wide, preferred_element_type=jnp.float32
    )
    heads_part = jnp.einsum(
        "td,hd->th", branch_wide, output_weight, preferred_element_type=jnp.float32
    )
    attended_grad = row_total(heads_part).astype(jnp.bfloat16)
    joined_grad = attend_back(
        joined_rows, slopes, log_sums, attended_grad.reshape(seq_count, SEQ_LEN, head_count, HD)
    )
    column_sums = jnp.sum(joined_grad.astype(jnp.float32), axis=(0, 1))
    query_value_bias_grad = jnp.stack([column_sums[:, 0], column_sums[:, 2]], axis=1).reshape(
        head_count, 2 * HD
    )
    joined_wide = row_gather(joined_grad.reshape(row_count, head_count * 3 * HD))
    joined_weight_grad = jnp.einsum(
        "td,tf->df", wide_first, joined_wide, preferred_element_type=jnp.float32
    )
    normed_first_grad = column_total(
        jnp.einsum("tf,df->td", joined_wide, joined_weight, preferred_element_type=jnp.float32)
    )
    back_first, first_gain_grad, first_shift_grad = norm_backward(
        normed_first_grad, centered_first, scale_first, first_gain, stats_total
    )
    tokens_grad = hidden_grad + back_first
    lower = (
        first_gain_grad,
        first_shift_grad,
        joined_weight_grad,
        query_value_bias_grad,
        output_weight_grad,
        output_bias_grad,
    )
    return (outcome.astype(jnp.bfloat16), tokens_grad, lower, upper)


def local(
    tokens,
    first_gain,
    first_shift,
    joined_weight,
    query_value_bias,
    output_weight,
    output_bias,
    second_gain,
    second_shift,
    up_weight,
    up_bias,
    down_weight,
    down_bias,
    out_grad,
):
    outcome, tokens_grad, lower, upper = blocks_layer(
        tokens,
        first_gain,
        first_shift,
        joined_weight,
        query_value_bias,
        output_weight,
        output_bias,
        second_gain,
        second_shift,
        up_weight,
        up_bias,
        down_weight,
        down_bias,
        out_grad,
    )
    (
        first_gain_grad,
        first_shift_grad,
        joined_weight_grad,
        query_value_bias_grad,
        output_weight_grad,
        output_bias_grad,
    ) = lower
    (
        down_weight_grad,
        down_bias_grad,
        up_weight_grad,
        up_bias_grad,
        second_gain_grad,
        second_shift_grad,
    ) = upper
    (
        first_gain_grad,
        first_shift_grad,
        joined_weight_grad,
        query_value_bias_grad,
        output_weight_grad,
        output_bias_grad,
        second_gain_grad,
        second_shift_grad,
        up_weight_grad,
        up_bias_grad,
        down_weight_grad,
        down_bias_grad,
    ) = lax.psum(
        (
            first_gain_grad,
            first_shift_grad,
            joined_weight_grad,
            query_value_bias_grad,
            output_weight_grad,
            output_bias_grad,
            second_gain_grad,
            second_shift_grad,
            up_weight_grad,
            up_bias_grad,
            down_weight_grad,
            down_bias_grad,
        ),
        "dp",
    )
    return (
        outcome,
        tokens_grad,
        first_gain_grad,
        first_shift_grad,
        joined_weight_grad,
        query_value_bias_grad,
        output_weight_grad,
        output_bias_grad,
        second_gain_grad,
        second_shift_grad,
        up_weight_grad,
        up_bias_grad,
        down_weight_grad,
        down_bias_grad,
    )


def solution(mesh):
    in_specs = (
        P("dp", ("row", "col")),
        P(("row", "col")),
        P(("row", "col")),
        P("row", "col"),
        P(("col", "row"), None),
        P("col", "row"),
        P(("row", "col")),
        P(("row", "col")),
        P(("row", "col")),
        P("row", "col"),
        P(("col", "row")),
        P("col", "row"),
        P(("row", "col")),
        P("dp", ("row", "col")),
    )
    out_specs = (
        P("dp", ("row", "col")),
        P("dp", ("row", "col")),
        P(("row", "col")),
        P(("row", "col")),
        P("row", "col"),
        P(("col", "row"), None),
        P("col", "row"),
        P(("row", "col")),
        P(("row", "col")),
        P(("row", "col")),
        P("row", "col"),
        P(("col", "row")),
        P("col", "row"),
        P(("row", "col")),
    )
    return jax.shard_map(local, mesh=mesh, in_specs=in_specs, out_specs=out_specs, check_vma=False)
```

profile of v0, /device:TPU:0, one launch (start us, length us, event | category | flops | bytes accessed | tf_op | source)
XLA Modules:
  0.0 1704.9 jit_solution(9988571142799861904)
XLA Ops:
  10.1 14.3 all-reduce.7
  28.6 57.8 %all-gather.9.cloned.1.call-done = bf16[4096,512]{1,0:T(8,128)(2,1)} async-done(((bf16[4096,256]{1,0:T(8,128)(2,1)}), bf16[4096,512]{1,0:T(8,128)(2,1)}) %all-gather.9.cloned.1.call-update) | async-done | bytes 4194320 | tf_op jit(solution)/shard_map/all_gather | solution.py:23
  110.1 25.7 %reduce-scatter.9.cloned.1.call-done = f32[4096,768]{1,0:T(8,128)} async-done(((f32[4096,1536]{1,0:T(8,128)}), f32[4096,768]{1,0:T(8,128)}) %reduce-scatter.9.cloned.1.call-update) | async-done | bytes 12582928 | tf_op jit(solution)/shard_map/reduce_scatter | solution.py:35
  175.4 18.0 %fusion.62 = (f32[4,4,512]{2,1,0:T(4,128)S(1)}, f32[4,4,512,1024]{3,2,1,0:T(8,128)}) fusion(f32[4,512,1024]{2,1,0:T(8,128)} %broadcast_multiply_fusion, bf16[4,1024,4,1,64]{1,0,4,3,2:T(4,128)(2,1)} %copy-done.5, bf16[4,1024,4,64]{1,3,2,0:T(8,128)(2,1)} %get-tuple-element.142, pred[512,1024]{1,0:T(8,128)(4,1)S(1)} %broadcast_compare_fusion), kind=kOutput, calls=%fused_computation.117 | convolution fusion | flops 1107288064 | bytes 45645824 | tf_op jit(solution)/shard_map/sqhd,skhd->shqk/dot_general | solution.py:72
  193.4 14.3 fusion
  207.8 15.1 fusion.42
  251.0 14.9 all-gather.11.cloned.1.call-done
  274.6 99.7 %reduce-scatter.11.cloned.1.call-done = f32[4096,256]{1,0:T(8,128)} async-done(((f32[4096,512]{1,0:T(8,128)}), f32[4096,256]{1,0:T(8,128)}) %reduce-scatter.11.cloned.1.call-update) | async-done | bytes 4194320 | tf_op jit(solution)/shard_map/reduce_scatter | solution.py:27
  395.9 37.1 %all-gather.17.cloned.1.call-done = bf16[4096,512]{1,0:T(8,128)(2,1)} async-done(((bf16[4096,256]{1,0:T(8,128)(2,1)}), bf16[4096,512]{1,0:T(8,128)(2,1)}) %all-gather.17.cloned.1.call-update) | async-done | bytes 4194320 | tf_op jit(solution)/shard_map/all_gather | solution.py:23
  433.0 19.5 %fusion.68 = f32[4096,2048]{1,0:T(8,128)} fusion(bf16[4096,512]{1,0:T(8,128)(2,1)} %all-gather.17.cloned.1.call-done, bf16[2048,512]{1,0:T(8,128)(2,1)} %param.37), kind=kOutput, calls=%fused_computation.123 | convolution fusion | flops 8589934592 | bytes 39845888 | tf_op jit(solution)/shard_map/td,fd->tf/dot_general | solution.py:216
  452.7 39.2 %all-gather.13.cloned.1.call-done = bf16[4096,512]{1,0:T(8,128)(2,1)} async-done(((bf16[4096,256]{1,0:T(8,128)(2,1)}), bf16[4096,512]{1,0:T(8,128)(2,1)}) %all-gather.13.cloned.1.call-update) | async-done | bytes 4194320 | tf_op jit(solution)/shard_map/all_gather | solution.py:23
  491.9 24.7 %fusion.66 = f32[4096,2048]{1,0:T(8,128)} fusion(bf16[4096,512]{1,0:T(8,128)(2,1)} %all-gather.13.cloned.1.call-done, bf16[512,2048]{1,0:T(8,128)(2,1)S(1)} %copy-done), kind=kOutput, calls=%fused_computation.121 | convolution fusion | flops 8589934592 | bytes 39845888 | tf_op jit(solution)/shard_map/dot_general | solution.py:201
  517.1 22.4 %reduce-scatter.17.cloned.1.call-done = f32[4096,1024]{1,0:T(8,128)} async-done(((f32[4096,2048]{1,0:T(8,128)}), f32[4096,1024]{1,0:T(8,128)}) %reduce-scatter.17.cloned.1.call-update) | async-done | bytes 16777232 | tf_op jit(solution)/shard_map/reduce_scatter | solution.py:35
  539.5 48.8 %reduce-scatter.13.cloned.1.call-done = f32[4096,1024]{1,0:T(8,128)} async-done(((f32[4096,2048]{1,0:T(8,128)}), f32[4096,1024]{1,0:T(8,128)}) %reduce-scatter.13.cloned.1.call-update) | async-done | bytes 16777232 | tf_op jit(solution)/shard_map/reduce_scatter | solution.py:35
  588.3 22.4 %convert_reduce_fusion = (f32[1024]{0:T(1024)}, bf16[4096,1024]{1,0:T(8,128)(2,1)}, bf16[4096,1024]{1,0:T(8,128)(2,1)}) fusion(f32[4096,1024]{1,0:T(8,128)} %reduce-scatter.17.cloned.1.call-done, f32[4096,1024]{1,0:T(8,128)} %reduce-scatter.13.cloned.1.call-done, f32[1024]{0:T(1024)S(1)} %copy-done.41), kind=kLoop, calls=%fused_computation.18 | loop fusion | flops 104856576 | bytes 50339840 | tf_op jit(solution)/shard_map/reduce_sum | solution.py:220
  611.4 30.8 %all-gather.19.cloned.1.call-done = bf16[4096,2048]{1,0:T(8,128)(2,1)} async-done(((bf16[4096,1024]{1,0:T(8,128)(2,1)}), bf16[4096,2048]{1,0:T(8,128)(2,1)}) %all-gather.19.cloned.1.call-update) | async-done | bytes 16777232 | tf_op jit(solution)/shard_map/all_gather | solution.py:31
  642.2 15.3 fusion.69
  657.5 17.4 %all-gather.15.cloned.1.call-done = bf16[4096,2048]{1,0:T(8,128)(2,1)} async-done(((bf16[4096,1024]{1,0:T(8,128)(2,1)}), bf16[4096,2048]{1,0:T(8,128)(2,1)}) %all-gather.15.cloned.1.call-update) | async-done | bytes 16777232 | tf_op jit(solution)/shard_map/all_gather | solution.py:31
  674.9 14.4 fusion.67
  689.6 88.2 %reduce-scatter.19.cloned.1.call-done = f32[4096,256]{1,0:T(8,128)} async-done(((f32[4096,512]{1,0:T(8,128)}), f32[4096,256]{1,0:T(8,128)}) %reduce-scatter.19.cloned.1.call-update) | async-done | bytes 4194320 | tf_op jit(solution)/shard_map/reduce_scatter | solution.py:27
  795.7 84.4 %reduce-scatter.15.cloned.1.call-done = f32[4096,256]{1,0:T(8,128)} async-done(((f32[4096,512]{1,0:T(8,128)}), f32[4096,256]{1,0:T(8,128)}) %reduce-scatter.15.cloned.1.call-update) | async-done | bytes 4194320 | tf_op jit(solution)/shard_map/reduce_scatter | solution.py:27
  892.5 56.8 %all-gather.21.cloned.1.call-done = bf16[4096,512]{1,0:T(8,128)(2,1)} async-done(((bf16[4096,256]{1,0:T(8,128)(2,1)}), bf16[4096,512]{1,0:T(8,128)(2,1)}) %all-gather.21.cloned.1.call-update) | async-done | bytes 4194320 | tf_op jit(solution)/shard_map/all_gather | solution.py:23
  957.9 16.2 reduce-scatter.21.cloned.1.call-done
  1029.3 22.5 %multiply_reduce_fusion = (f32[4,4,512]{2,1,0:T(4,128)S(1)}, f32[4,4,512,1024]{3,2,1,0:T(8,128)}) fusion(f32[4,4,512,1024]{3,2,1,0:T(8,128)} %get-tuple-element.134, f32[4,4,512]{2,1,0:T(4,128)S(1)} %bitcast.98, bf16[4,512,4,64]{1,3,2,0:T(8,128)(2,1)S(1)} %copy.87, bf16[4,1024,4,1,64]{1,0,4,3,2:T(4,128)(2,1)S(1)} %copy-done.11), kind=kOutput, calls=%fused_computation.1 | convolution fusion | flops 1098899456 | bytes 70320128 | tf_op jit(solution)/shard_map/sqhd,skhd->shqk/dot_general | solution.py:125
  1051.8 15.4 fusion.33
  1067.2 27.9 %multiply_convert_fusion = bf16[4,4,512,1024]{3,2,1,0:T(8,128)(2,1)} fusion(f32[4,4,512,1024]{3,2,1,0:T(8,128)} %get-tuple-element.140, f32[4,4,512,1024]{3,2,1,0:T(8,128)} %get-tuple-element.134, f32[4,4,512]{2,1,0:T(4,128)S(1)} %get-tuple-element.139, f32[4,4,512]{2,1,0:T(4,128)S(1)} %bitcast.100), kind=kLoop, calls=%fused_computation | loop fusion | flops 33554432 | bytes 83951616 | tf_op jit(solution)/shard_map/convert_element_type | solution.py:130
  1141.3 26.3 %all-gather.23.cloned.1.call-done = bf16[4096,1536]{0,1:T(8,128)(2,1)} async-done(((bf16[4096,768]{0,1:T(8,128)(2,1)}), bf16[4096,1536]{0,1:T(8,128)(2,1)}) %all-gather.23.cloned.1.call-update) | async-done | bytes 12582928 | tf_op jit(solution)/shard_map/all_gather | solution.py:31
  1179.6 15.1 fusion.74
  1194.7 14.5 fusion.75
  1221.5 58.6 %reduce-scatter.23.cloned.1.call-done = f32[4096,256]{1,0:T(8,128)} async-done(((f32[4096,512]{1,0:T(8,128)}), f32[4096,256]{1,0:T(8,128)}) %reduce-scatter.23.cloned.1.call-update) | async-done | bytes 4194320 | tf_op jit(solution)/shard_map/reduce_scatter | solution.py:27
  1284.7 38.6 %all-reduce.2 = (f32[256]{0:T(256)}, f32[256]{0:T(256)}, f32[4,128]{1,0:T(4,128)}, f32[256]{0:T(256)}, f32[256]{0:T(256)}, /*index=5*/f32[256]{0:T(256)}, f32[1024]{0:T(1024)}, f32[256]{0:T(256)}) all-reduce(f32[256]{0:T(256)S(1)} %get-tuple-element.80, ...), channel_id=1, replica_groups=mesh['dp'=8,'row'=2,'col'=2] {'dp'}, use_global_device_ids=true, to_apply=%region_31.32 | all-reduce | flops 3072 | bytes 24576 | tf_op jit(solution)/shard_map/psum | solution.py:339
  1344.1 343.5 %all-reduce.10.cloned.1.call-done = (f32[512,1536]{1,0:T(8,128)}, f32[512,512]{1,0:T(8,128)}, f32[512,2048]{1,0:T(8,128)}, f32[2048,512]{1,0:T(8,128)}) async-done(((f32[512,1536]{1,0:T(8,128)}, f32[512,512]{1,0:T(8,128)}, f32[512,2048]{1,0:T(8,128)}, f32[2048,512]{1,0:T(8,128)}), (f32[512,1536]{1,0:T(8,128)}, f32[512,512]{1,0:T(8,128)}, f32[512,2048]{1,0:T(8,128)}, ...) | async-done | bytes 12582928 | tf_op jit(solution)/shard_map/psum | solution.py:339
  (216 shorter events, 330.3 us)
Async XLA Ops:
  7.2 484.7 %copy-start = (bf16[512,2048]{1,0:T(8,128)(2,1)S(1)}, bf16[512,2048]{1,0:T(8,128)(2,1)}, u32[]{:S(2)}) copy-start(bf16[512,2048]{1,0:T(8,128)(2,1)} %param.35) | copy-start | bytes 6291460
  7.2 79.2 %all-gather.9.cloned.1.call-start = ((), (), s32[]{:S(2)}) async-start(), calls=%async_computation.8 | async-start | bytes 6291456 | tf_op jit(solution)/shard_map/all_gather | solution.py:23
  28.6 107.2 %reduce-scatter.9.cloned.1.call-start = ((), (), s32[]{:S(2)}) async-start(), calls=%async_computation.9 | async-start | bytes 37748736 | tf_op jit(solution)/shard_map/reduce_scatter | solution.py:35
  100.2 165.7 %all-gather.11.cloned.1.call-start = ((), (), s32[]{:S(2)}) async-start(), calls=%async_computation.10 | async-start | bytes 6291456 | tf_op jit(solution)/shard_map/all_gather | solution.py:31
  250.9 123.4 %reduce-scatter.11.cloned.1.call-start = ((), (), s32[]{:S(2)}) async-start(), calls=%async_computation.11 | async-start | bytes 12582912 | tf_op jit(solution)/shard_map/reduce_scatter | solution.py:27
  273.7 100.6 %copy-start.45 = (f32[256]{0:T(256)S(1)}, f32[256]{0:T(256)}, u32[]{:S(2)}) copy-start(f32[256]{0:T(256)} %param.32) | copy-start | bytes 3076
  273.7 159.3 %all-gather.17.cloned.1.call-start = ((), (), s32[]{:S(2)}) async-start(), calls=%async_computation.16 | async-start | bytes 6291456 | tf_op jit(solution)/shard_map/all_gather | solution.py:23
  274.3 117.6 %copy-start.35 = (f32[256]{0:T(256)S(1)}, f32[256]{0:T(256)}, u32[]{:S(2)}) copy-start(f32[256]{0:T(256)} %param.33) | copy-start | bytes 3076
  274.3 117.6 %copy-start.43 = (f32[256]{0:T(256)S(1)}, f32[256]{0:T(256)}, u32[]{:S(2)}) copy-start(f32[256]{0:T(256)} %param.34) | copy-start | bytes 3076
  274.4 217.5 %all-gather.13.cloned.1.call-start = ((), (), s32[]{:S(2)}) async-start(), calls=%async_computation.12 | async-start | bytes 6291456 | tf_op jit(solution)/shard_map/all_gather | solution.py:23
  395.9 143.6 %reduce-scatter.17.cloned.1.call-start = ((), (), s32[]{:S(2)}) async-start(), calls=%async_computation.17 | async-start | bytes 50331648 | tf_op jit(solution)/shard_map/reduce_scatter | solution.py:35
  452.6 135.7 %reduce-scatter.13.cloned.1.call-start = ((), (), s32[]{:S(2)}) async-start(), calls=%async_computation.13 | async-start | bytes 50331648 | tf_op jit(solution)/shard_map/reduce_scatter | solution.py:35
  516.6 71.7 %copy-start.41 = (f32[1024]{0:T(1024)S(1)}, f32[1024]{0:T(1024)}, u32[]{:S(2)}) copy-start(f32[1024]{0:T(1024)} %param.36) | copy-start | bytes 12292
  516.6 125.5 %all-gather.19.cloned.1.call-start = ((), (), s32[]{:S(2)}) async-start(), calls=%async_computation.18 | async-start | bytes 25165824 | tf_op jit(solution)/shard_map/all_gather | solution.py:31
  610.8 64.2 %all-gather.15.cloned.1.call-start = ((), (), s32[]{:S(2)}) async-start(), calls=%async_computation.14 | async-start | bytes 25165824 | tf_op jit(solution)/shard_map/all_gather | solution.py:31
  611.3 166.4 %reduce-scatter.19.cloned.1.call-start = ((), (), s32[]{:S(2)}) async-start(), calls=%async_computation.19 | async-start | bytes 12582912 | tf_op jit(solution)/shard_map/reduce_scatter | solution.py:27
  657.5 222.6 %reduce-scatter.15.cloned.1.call-start = ((), (), s32[]{:S(2)}) async-start(), calls=%async_computation.15 | async-start | bytes 12582912 | tf_op jit(solution)/shard_map/reduce_scatter | solution.py:27
  689.4 190.7 %copy-start.13 = (bf16[4096,256]{1,0:T(8,128)(2,1)S(1)}, bf16[4096,256]{1,0:T(8,128)(2,1)}, u32[]{:S(2)}) copy-start(bf16[4096,256]{1,0:T(8,128)(2,1)} %param.39) | copy-start | bytes 6291460
  689.4 190.7 %copy-start.44 = (f32[256]{0:T(256)S(1)}, f32[256]{0:T(256)}, u32[]{:S(2)}) copy-start(f32[256]{0:T(256)} %param.38) | copy-start | bytes 3076
  689.4 259.9 %all-gather.21.cloned.1.call-start = ((), (), s32[]{:S(2)}) async-start(), calls=%async_computation.20 | async-start | bytes 6291456 | tf_op jit(solution)/shard_map/all_gather | solution.py:23
  892.4 81.7 %reduce-scatter.21.cloned.1.call-start = ((), (), s32[]{:S(2)}) async-start(), calls=%async_computation.21 | async-start | bytes 12582912 | tf_op jit(solution)/shard_map/reduce_scatter | solution.py:35
  957.1 210.4 %all-gather.23.cloned.1.call-start = ((), (), s32[]{:S(2)}) async-start(), calls=%async_computation.22 | async-start | bytes 18874368 | tf_op jit(solution)/shard_map/all_gather | solution.py:31
  1141.2 138.8 %reduce-scatter.23.cloned.1.call-start = ((), (), s32[]{:S(2)}) async-start(), calls=%async_computation.23 | async-start | bytes 12582912 | tf_op jit(solution)/shard_map/reduce_scatter | solution.py:27
  1179.5 508.1 %all-reduce.10.cloned.1.call-start = ((), (), s32[]{:S(2)}) async-start(), calls=%async_computation.24 | async-start | bytes 25165824 | tf_op jit(solution)/shard_map/psum | solution.py:339
  1221.3 58.8 %copy-start.29 = (f32[4096]{0:T(1024)S(1)}, f32[4096]{0:T(1024)}, u32[]{:S(2)}) copy-start(f32[4096]{0:T(1024)} %copy-done.28) | copy-start | bytes 49156
  1221.3 58.8 %copy-start.31 = (f32[4096]{0:T(1024)S(1)}, f32[4096]{0:T(1024)}, u32[]{:S(2)}) copy-start(f32[4096]{0:T(1024)} %copy-done.30) | copy-start | bytes 49156
  1221.3 58.8 %copy-start.36 = (f32[256]{0:T(256)S(1)}, f32[256]{0:T(256)}, u32[]{:S(2)}) copy-start(f32[256]{0:T(256)} %param.27) | copy-start | bytes 3076
  1221.3 63.4 %copy-start.34 = (f32[1024]{0:T(1024)S(1)}, f32[1024]{0:T(1024)}, u32[]{:S(2)}) copy-start(f32[1024]{0:T(1024)} %get-tuple-element.110) | copy-start | bytes 12292
  1221.3 63.4 %copy-start.37 = (f32[256]{0:T(256)S(1)}, f32[256]{0:T(256)}, u32[]{:S(2)}) copy-start(f32[256]{0:T(256)} %get-tuple-element.78) | copy-start | bytes 3076
  1221.3 63.4 %copy-start.38 = (f32[256]{0:T(256)S(1)}, f32[256]{0:T(256)}, u32[]{:S(2)}) copy-start(f32[256]{0:T(256)} %get-tuple-element.84) | copy-start | bytes 3076
  1221.3 63.4 %copy-start.39 = (f32[256]{0:T(256)S(1)}, f32[256]{0:T(256)}, u32[]{:S(2)}) copy-start(f32[256]{0:T(256)} %get-tuple-element.112) | copy-start | bytes 3076
  1221.3 63.4 %copy-start.40 = (f32[256]{0:T(256)S(1)}, f32[256]{0:T(256)}, u32[]{:S(2)}) copy-start(f32[256]{0:T(256)} %get-tuple-element.124) | copy-start | bytes 3076
  (38 other events, 410.7 us)
Sparse Core Ops, SparseCore 0:
  28.7 57.6 all-gather.8
  100.3 35.4 reduce-scatter.8
  251.0 14.8 all-gather.10
  273.9 100.4 reduce-scatter.10
  375.8 57.2 all-gather.16
  435.1 56.7 all-gather.12
  494.3 45.1 reduce-scatter.16
  541.9 46.3 reduce-scatter.12
  610.9 31.2 all-gather.18
  643.6 31.2 all-gather.14
  677.3 100.4 reduce-scatter.18
  779.9 100.1 reduce-scatter.14
  892.6 56.6 all-gather.20
  957.3 16.7 reduce-scatter.20
  1141.4 26.1 all-gather.22
  1179.6 100.4 reduce-scatter.22
  1286.6 400.9 all-reduce.9
where the time goes:
time: 1710 us; the launch traced here: 1700 us
  waiting for transfers between devices  1070 us (63%)
  matrix products  291 us (17%)
  other arithmetic  153 us (9%)
  blocking collectives  90.3 us (5%)
  local copies, waits for them, and re-layouts  85.1 us (5%)
    psum x1, waiting for transfers between devices, local(): lax.psum((first_gain_grad, first_shift_grad, joined_weight_grad, query_va...  343 us
    reduce_scatter x4, waiting for transfers between devices, column_total(): lax.psum_scatter(partial_sums, 'col', scatter_dimension=1, tiled=True)  331 us
    all_gather x4, waiting for transfers between devices, column_gather(): return lax.all_gather(values, 'col', axis=1, tiled=True)  191 us
    reduce_scatter x4, waiting for transfers between devices, row_total(): lax.psum_scatter(partial_sums, 'row', scatter_dimension=1, tiled=True)  113 us
    all_gather x4, waiting for transfers between devices, row_gather(): return lax.all_gather(values, 'row', axis=1, tiled=True)  89.4 us
    psum x4, blocking collectives, stats_total(): return lax.psum((first, second), ('row', 'col'))  51.7 us
    convert_element_type x2, other arithmetic, attend_back(): score_grads = (chances * (prob_grads - jnp.sum(chances * prob_grads, axis...  40.1 us
    psum x1, blocking collectives, local(): lax.psum((first_gain_grad, first_shift_grad, joined_weight_grad, query_va...  38.6 us
  transfers between devices with their start and end apart: 17, of which 17 were waited for; matrix products, arithmetic and copies ran while one was open for 9% of the time, Pallas kernels for 0%

commit v1 on v0

v1 whole, which is shorter than its diff:
```python
import math
from functools import partial

import jax
import jax.numpy as jnp
from jax import lax
from jax.experimental import pallas as pl
from jax.experimental.pallas import tpu as pltpu
from jax.sharding import PartitionSpec as P

D = 1024
H = 16
HD = 64
FF = 4096
SEQ_LEN = 1024
QB = 256
EPSILON = 1e-05
L2E = math.log2(math.e)
BF = jnp.bfloat16
F32 = jnp.float32


def bdot(a, b, ca, cb):
    return lax.dot_general(a, b, (((ca,), (cb,)), ((), ())), preferred_element_type=F32)


def bias_cols(slope, n):
    j = lax.broadcasted_iota(jnp.int32, (n, HD), 0).astype(F32)
    lane = lax.broadcasted_iota(jnp.int32, (n, HD), 1)
    full = j * (slope * 8.0)
    hi = full.astype(BF)
    rest = full - hi.astype(F32)
    mid = rest.astype(BF)
    low = (rest - mid.astype(F32)).astype(BF)
    return jnp.where(lane == 0, hi, jnp.where(lane == 1, mid, jnp.where(lane == 2, low, jnp.zeros_like(hi))))


def block_scores(keys, queries, stop, i):
    z = bdot(keys[:stop], queries[i * QB : (i + 1) * QB], 1, 1) * (HD ** (-0.5) * L2E)
    row = lax.broadcasted_iota(jnp.int32, (QB, QB), 0)
    col = lax.broadcasted_iota(jnp.int32, (QB, QB), 1)
    last = jnp.where(row <= col, z[stop - QB :], -1e30)
    return last if stop == QB else jnp.concatenate([z[: stop - QB], last], 0)


def attend_kernel(slopes, x_ref, o_ref, lse_ref):
    n = x_ref.shape[0]
    pair = pl.program_id(0)
    ones = jnp.ones((n, HD), BF)
    heads = []
    for t in range(2):
        base = 3 * HD * t
        q, k, v = (x_ref[:, base + HD * s : base + HD * (s + 1)] for s in range(3))
        keys = jnp.concatenate([k, bias_cols(slopes[2 * pair + t], n)], 1)
        queries = jnp.concatenate([q, ones], 1)
        pieces = []
        for i in range(n // QB):
            stop = QB * (i + 1)
            z = block_scores(keys, queries, stop, i)
            top = jnp.max(z, 0, keepdims=True)
            p = jnp.exp2(z - top)
            total = jnp.sum(p, 0, keepdims=True)
            pieces.append((bdot(v[:stop], p.astype(BF), 0, 0) / total).T)
            lse_ref[0, t : t + 1, i * QB : stop] = top + jnp.log2(total)
        heads.append(jnp.concatenate(pieces, 0))
    o_ref[...] = jnp.concatenate(heads, 1).astype(BF)


def attend(slopes, joined):
    n, width = joined.shape
    pairs = width // (6 * HD)
    return pl.pallas_call(
        attend_kernel,
        grid_spec=pltpu.PrefetchScalarGridSpec(
            num_scalar_prefetch=1,
            grid=(pairs,),
            in_specs=[pl.BlockSpec((n, 6 * HD), lambda h, s: (0, h))],
            out_specs=[
                pl.BlockSpec((n, 2 * HD), lambda h, s: (0, h)),
                pl.BlockSpec((1, 2, n), lambda h, s: (h, 0, 0)),
            ],
        ),
        out_shape=[
            jax.ShapeDtypeStruct((n, pairs * 2 * HD), BF),
            jax.ShapeDtypeStruct((pairs, 2, n), F32),
        ],
        compiler_params=pltpu.CompilerParams(vmem_limit_bytes=40 << 20),
        cost_estimate=pl.CostEstimate(
            flops=32 * n * n * HD * pairs, bytes_accessed=n * 512 * pairs * 2, transcendentals=n * n * pairs
        ),
        name="attend",
    )(slopes, joined)


def attend_back_kernel(slopes, x_ref, do_ref, lse_ref, dx_ref, dk_ref, dv_ref):
    n = x_ref.shape[0]
    pair = pl.program_id(0)
    ones = jnp.ones((n, HD), BF)
    parts = []
    for t in range(2):
        base = 3 * HD * t
        q, k, v = (x_ref[:, base + HD * s : base + HD * (s + 1)] for s in range(3))
        do = do_ref[:, HD * t : HD * (t + 1)]
        keys = jnp.concatenate([k, bias_cols(slopes[2 * pair + t], n)], 1)
        queries = jnp.concatenate([q, ones], 1)
        dq = []
        for i in reversed(range(n // QB)):
            stop = QB * (i + 1)
            rows = slice(i * QB, stop)
            z = block_scores(keys, queries, stop, i)
            p = jnp.exp2(z - lse_ref[0, t : t + 1, rows])
            dp = bdot(v[:stop], do[rows], 1, 1)
            total = jnp.sum(p * dp, 0, keepdims=True)
            ds = (p * (dp - total)).astype(BF)
            dq.append(bdot(k[:stop], ds, 0, 0).T)
            dk = bdot(ds, q[rows], 1, 0)
            dv = bdot(p.astype(BF), do[rows], 1, 0)
            if stop == n:
                dk_ref[...] = dk
                dv_ref[...] = dv
            else:
                dk_ref[:stop] += dk
                dv_ref[:stop] += dv
        scale = HD ** (-0.5)
        parts += [jnp.concatenate(dq[::-1], 0) * scale, dk_ref[...] * scale, dv_ref[...]]
    dx_ref[...] = jnp.concatenate(parts, 1).astype(BF)


def attend_back(slopes, joined, out_grads, lse):
    n, width = joined.shape
    pairs = width // (6 * HD)
    return pl.pallas_call(
        attend_back_kernel,
        grid_spec=pltpu.PrefetchScalarGridSpec(
            num_scalar_prefetch=1,
            grid=(pairs,),
            in_specs=[
                pl.BlockSpec((n, 6 * HD), lambda h, s: (0, h)),
                pl.BlockSpec((n, 2 * HD), lambda h, s: (0, h)),
                pl.BlockSpec((1, 2, n), lambda h, s: (h, 0, 0)),
            ],
            out_specs=pl.BlockSpec((n, 6 * HD), lambda h, s: (0, h)),
            scratch_shapes=[pltpu.VMEM((n, HD), F32)] * 2,
        ),
        out_shape=jax.ShapeDtypeStruct(joined.shape, BF),
        compiler_params=pltpu.CompilerParams(vmem_limit_bytes=40 << 20),
        cost_estimate=pl.CostEstimate(
            flops=80 * n * n * HD * pairs, bytes_accessed=n * 1024 * pairs * 2, transcendentals=n * n * pairs
        ),
        name="attend_back",
    )(slopes, joined, out_grads, lse)


def swap(values, axis):
    return lax.ppermute(values, axis, [(0, 1), (1, 0)])


def mesh_bits(count):
    return [1 << b for b in range(count.bit_length() - 1)]


def side_by_side(flag, mine, other, axis):
    return jnp.where(
        flag, jnp.concatenate([other, mine], axis), jnp.concatenate([mine, other], axis)
    )


def to_sequence(block, row, col):
    n, width = block.shape
    parts = block.reshape(2, 2, n // 4, width)
    own = lax.dynamic_index_in_dim(parts, col, 1, False)
    got = swap(lax.dynamic_index_in_dim(parts, 1 - col, 1, False), "col")
    half = side_by_side(col == 1, own, got, 2)
    mine = lax.dynamic_index_in_dim(half, row, 0, False)
    other = swap(lax.dynamic_index_in_dim(half, 1 - row, 0, False), "row")
    return jnp.concatenate([mine, other], 1)


def from_sequence(values, row, col):
    n, width = values.shape
    mine, send = values[:, : width // 2], values[:, width // 2 :]
    got = swap(send, "row")
    half = jnp.where(row == 1, jnp.stack([got, mine]), jnp.stack([mine, got]))
    parts = half.reshape(2, n, 2, width // 4)
    own = lax.dynamic_index_in_dim(parts, col, 2, False)
    got = swap(lax.dynamic_index_in_dim(parts, 1 - col, 2, False), "col")
    return side_by_side(col == 1, own[:, None], got[:, None], 1).reshape(4 * n, width // 4)


def whole_weight(block):
    across = swap(block, "col")
    return block, across, swap(block, "row"), swap(across, "row")


def put(quarters, row_dim):
    own, across, below, both = quarters
    if row_dim == 0:
        return jnp.concatenate([jnp.concatenate([own, across], 1), jnp.concatenate([below, both], 1)], 0)
    return jnp.concatenate([jnp.concatenate([own, below], 1), jnp.concatenate([across, both], 1)], 0)


def halves(values, dim):
    n = values.shape[dim] // 2
    return lax.slice_in_dim(values, 0, n, axis=dim), lax.slice_in_dim(values, n, 2 * n, axis=dim)


def reduce_weight(grad, row_dim, dp_size):
    mine, send = halves(grad, row_dim)
    mine = mine.astype(F32) + swap(send.astype(BF), "row").astype(F32)
    mine, send = halves(mine, 1 - row_dim)
    mine = mine + swap(send.astype(BF), "col").astype(F32)
    place = lax.axis_index("dp")
    bits = mesh_bits(dp_size)
    for bit in bits:
        upper = (place // bit) % 2 == 1
        low, high = halves(mine, 0)
        send = jnp.where(upper, low, high).astype(BF)
        mine = jnp.where(upper, high, low) + lax.ppermute(
            send, "dp", [(i, i ^ bit) for i in range(dp_size)]
        ).astype(F32)
    mine = mine.astype(BF)
    for bit in bits[::-1]:
        upper = (place // bit) % 2 == 1
        got = lax.ppermute(mine, "dp", [(i, i ^ bit) for i in range(dp_size)])
        mine = side_by_side(upper, mine, got, 0)
    return mine.astype(F32)


def normed(values, gain, shift):
    average = jnp.mean(values, axis=1, keepdims=True)
    away = values - average
    scale = lax.rsqrt(jnp.mean(away * away, axis=1, keepdims=True) + EPSILON)
    centered = away * scale
    return centered, scale, (centered * gain + shift).astype(BF)


def norm_backward(upstream, centered, scale, gain):
    scaled = upstream * gain
    back = scale * (
        scaled
        - jnp.mean(scaled, axis=1, keepdims=True)
        - centered * jnp.mean(scaled * centered, axis=1, keepdims=True)
    )
    return back, jnp.sum(upstream * centered, axis=0), jnp.sum(upstream, axis=0)


def local(
    dp_size,
    tokens,
    first_gain,
    first_shift,
    joined_weight,
    query_value_bias,
    output_weight,
    output_bias,
    second_gain,
    second_shift,
    up_weight,
    up_bias,
    down_weight,
    down_bias,
    out_grad,
):
    row, col = lax.axis_index("row"), lax.axis_index("col")
    heads = query_value_bias.shape[0] * 4
    small = jnp.concatenate(
        [
            first_gain,
            first_shift,
            output_bias,
            second_gain,
            second_shift,
            down_bias,
            up_bias,
            query_value_bias.reshape(-1),
        ]
    )
    by_row = jnp.stack([small, swap(small, "row")])
    small = jnp.stack([by_row, swap(by_row, "col")], 1)

    def feature_vector(k):
        part = small[:, :, 256 * k : 256 * (k + 1)]
        part = jnp.where(col == 1, part[:, ::-1], part)
        return part.reshape(-1)

    def hidden_vector(start, size):
        part = small[:, :, start : start + size]
        part = jnp.where(row == 1, part[::-1], part)
        return part.transpose(1, 0, 2).reshape(-1)

    g1, s1, ob, g2, s2, db = (feature_vector(k) for k in range(6))
    ub = hidden_vector(6 * 256, up_bias.shape[0])
    pair_bias = hidden_vector(6 * 256 + up_bias.shape[0], query_value_bias.size).reshape(heads, 2, HD)
    qv_bias = jnp.concatenate(
        [pair_bias[:, :1], jnp.zeros((heads, 1, HD), F32), pair_bias[:, 1:]], axis=1
    ).reshape(-1)
    head_ids = (jnp.arange(heads) + col * (heads // 2)) % heads
    slopes = jnp.exp2(-8.0 * (head_ids.astype(F32) + 1.0) / heads)

    inputs = to_sequence(tokens, row, col).astype(F32)
    wj = put(whole_weight(joined_weight), 0)
    wo = put(whole_weight(output_weight), 1)
    wu = put(whole_weight(up_weight), 0)
    og = to_sequence(out_grad, row, col)
    wd = put(whole_weight(down_weight), 1)

    centered_first, scale_first, normed_first = normed(inputs, g1, s1)
    joined = (jnp.dot(normed_first, wj, preferred_element_type=F32) + qv_bias).astype(BF)
    attended, lse = attend(slopes, joined)
    hidden = inputs + jnp.dot(attended, wo, preferred_element_type=F32) + ob
    centered_second, scale_second, normed_second = normed(hidden, g2, s2)
    preact = jnp.dot(normed_second, wu, preferred_element_type=F32) + ub
    activated = jax.nn.gelu(preact, approximate=True).astype(BF)
    outcome = hidden + jnp.dot(activated, wd, preferred_element_type=F32) + db
    result = from_sequence(outcome.astype(BF), row, col)

    upstream = og.astype(F32)
    down_bias_grad = jnp.sum(upstream, axis=0)
    down_weight_grad = reduce_weight(bdot(activated, og, 0, 0).astype(BF), 1, dp_size)
    activated_grad = bdot(og, wd, 1, 1)
    _, gelu_pull = jax.vjp(partial(jax.nn.gelu, approximate=True), preact)
    preact_grad = gelu_pull(activated_grad)[0].astype(BF)
    up_bias_grad = jnp.sum(preact_grad.astype(F32), axis=0)
    up_weight_grad = reduce_weight(bdot(normed_second, preact_grad, 0, 0).astype(BF), 0, dp_size)
    normed_second_grad = bdot(preact_grad, wu, 1, 1)
    back_second, second_gain_grad, second_shift_grad = norm_backward(
        normed_second_grad, centered_second, scale_second, g2
    )
    hidden_grad = upstream + back_second
    output_bias_grad = jnp.sum(hidden_grad, axis=0)
    branch = hidden_grad.astype(BF)
    output_weight_grad = reduce_weight(bdot(attended, branch, 0, 0).astype(BF), 1, dp_size)
    attended_grad = bdot(branch, wo, 1, 1).astype(BF)
    joined_grad = attend_back(slopes, joined, attended_grad, lse)
    column_sums = jnp.sum(joined_grad.astype(F32), axis=0).reshape(heads, 3, HD)
    query_value_bias_grad = jnp.stack([column_sums[:, 0], column_sums[:, 2]], axis=1).reshape(-1)
    joined_weight_grad = reduce_weight(bdot(normed_first, joined_grad, 0, 0).astype(BF), 0, dp_size)
    normed_first_grad = bdot(joined_grad, wj, 1, 1)
    back_first, first_gain_grad, first_shift_grad = norm_backward(
        normed_first_grad, centered_first, scale_first, g1
    )
    tokens_grad = from_sequence((hidden_grad + back_first).astype(BF), row, col).astype(F32)

    features = jnp.stack(
        [
            first_gain_grad,
            first_shift_grad,
            output_bias_grad,
            second_gain_grad,
            second_shift_grad,
            down_bias_grad,
        ]
    ).reshape(6, 2, 2, D // 4)
    features = jnp.where(col == 1, features[:, :, ::-1], features)
    features = features.transpose(1, 2, 0, 3).reshape(2, 2, -1)

    def hidden_parts(values):
        values = values.reshape(2, 2, -1)
        values = jnp.where(row == 1, values[:, ::-1], values)
        return values.transpose(1, 0, 2)

    totals = jnp.concatenate(
        [features, hidden_parts(up_bias_grad), hidden_parts(query_value_bias_grad)], 2
    )
    totals = totals[0] + swap(totals[1], "row")
    totals = totals[0] + swap(totals[1], "col")
    for bit in mesh_bits(dp_size):
        totals = totals + lax.ppermute(totals, "dp", [(i, i ^ bit) for i in range(dp_size)])
    w = D // 4
    fg, fs, obg, sg, ss, dbg = (totals[w * k : w * (k + 1)] for k in range(6))
    ubg = totals[6 * w : 6 * w + up_bias.shape[0]]
    qvg = totals[6 * w + up_bias.shape[0] :].reshape(query_value_bias.shape)
    return (
        result,
        tokens_grad,
        fg,
        fs,
        joined_weight_grad,
        qvg,
        output_weight_grad,
        obg,
        sg,
        ss,
        up_weight_grad,
        ubg,
        down_weight_grad,
        dbg,
    )


def solution(mesh):
    feature = P(("row", "col"))
    in_specs = (
        P("dp", ("row", "col")),
        feature,
        feature,
        P("row", "col"),
        P(("col", "row"), None),
        P("col", "row"),
        feature,
        feature,
        feature,
        P("row", "col"),
        P(("col", "row")),
        P("col", "row"),
        feature,
        P("dp", ("row", "col")),
    )
    out_specs = (
        P("dp", ("row", "col")),
        P("dp", ("row", "col")),
        feature,
        feature,
        P("row", "col"),
        P(("col", "row"), None),
        P("col", "row"),
        feature,
        feature,
        feature,
        P("row", "col"),
        P(("col", "row")),
        P("col", "row"),
        feature,
    )
    return jax.shard_map(
        partial(local, mesh.shape["dp"]),
        mesh=mesh,
        in_specs=in_specs,
        out_specs=out_specs,
        check_vma=False,
    )
```

time: 1710 us -> 783 us (0.46)
  waiting for transfers between devices: 1070 us -> 350 us
  matrix products: 291 us -> 175 us
  other arithmetic: 153 us -> 58.5 us
  blocking collectives: 90.3 us -> 0 us
  Pallas kernels: 0 us -> 81.5 us
  starting transfers between devices: 1.55 us -> 49.3 us
  local copies, waits for them, and re-layouts: 85.1 us -> 61.3 us
    reduce_scatter x8 -> x0, waiting for transfers between devices: 444 us -> none  [the longest x4 331 us: column_total(): lax.psum_scatter(partial_sums, 'col', scatter_dimension=1, tiled=True)]
    ppermute x0 -> x59, waiting for transfers between devices: none -> 350 us  [the longest x32 210 us: swap(): return lax.ppermute(values, axis, [(0, 1), (1, 0)])]
    psum x1 -> x0, waiting for transfers between devices: 343 us -> none  [local(): lax.psum((first_gain_grad, first_shift_grad, joined_weight_grad, query_va...]
    all_gather x8 -> x0, waiting for transfers between devices: 280 us -> none  [the longest x4 191 us: column_gather(): return lax.all_gather(values, 'col', axis=1, tiled=True)]
    dot_general x24 -> x12, matrix products: 291 us -> 175 us  [the longest x8 117 us: bdot(): lax.dot_general(a, b, (((ca,), (cb,)), ((), ())), preferred_element_type=...]
    psum x5 -> x0, blocking collectives: 90.3 us -> none  [the longest x4 51.7 us: stats_total(): return lax.psum((first, second), ('row', 'col'))]
    pallas_call x0 -> x2, Pallas kernels: none -> 81.5 us  [the longest x1 49.7 us: attend_back(): pl.pallas_call(attend_back_kernel, grid_spec=pltpu.PrefetchScalarGridSpec...]
    reduce_sum x9 -> x5, other arithmetic: 75.9 us -> 7.93 us  [the longest x1 5.56 us: local(): output_bias_grad = jnp.sum(hidden_grad, axis=0)]
  transfers between devices with their start and end apart: 17 -> 59, of which waited for: 17 -> 21; matrix products, arithmetic and copies ran while one was open for 9% -> 26% of each run, Pallas kernels for 0% -> 4%
where the time goes in v1:
time: 783 us; the launch traced here: 778 us
  waiting for transfers between devices  350 us (45%)
  matrix products  175 us (22%)
  Pallas kernels  81.5 us (10%)
  local copies, waits for them, and re-layouts  61.3 us (8%)
  other arithmetic  58.5 us (7%)
  starting transfers between devices  49.3 us (6%)
    ppermute x32, waiting for transfers between devices, swap(): return lax.ppermute(values, axis, [(0, 1), (1, 0)])  210 us
    dot_general x8, matrix products, bdot(): lax.dot_general(a, b, (((ca,), (cb,)), ((), ())), preferred_element_type=...  117 us
    ppermute x12, waiting for transfers between devices, reduce_weight(): got = lax.ppermute(mine, 'dp', [(i, i ^ bit) for i in range(dp_size)])  74.3 us
    ppermute x12, waiting for transfers between devices, reduce_weight(): lax.ppermute(send, 'dp', [(i, i ^ bit) for i in range(dp_size)]).astype(F32)  66.5 us
    pallas_call x1, Pallas kernels, attend_back(): pl.pallas_call(attend_back_kernel, grid_spec=pltpu.PrefetchScalarGridSpec...  49.7 us
    pallas_call x1, Pallas kernels, attend(): pl.pallas_call(attend_kernel, grid_spec=pltpu.PrefetchScalarGridSpec(num_...  31.8 us
    ppermute x32, starting transfers between devices, swap(): return lax.ppermute(values, axis, [(0, 1), (1, 0)])  22.3 us
    dot_general x1, matrix products, local(): outcome = hidden + jnp.dot(activated, wd, preferred_element_type=F32) + db  21.9 us
  transfers between devices with their start and end apart: 59, of which 21 were waited for; matrix products, arithmetic and copies ran while one was open for 26% of the time, Pallas kernels for 4%

profile of v1, /device:TPU:0, one launch (start us, length us, event | category | flops | bytes accessed | tf_op | source)
XLA Modules:
  0.0 778.4 jit_solution(2278428714882219197)
XLA Ops:
  21.9 84.3 %collective-permute-done.3 = f32[2,3072]{1,0:T(2,128)S(1)} collective-permute-done((f32[2,3072]{1,0:T(2,128)S(1)}, f32[2,3072]{1,0:T(2,128)S(1)}, u32[]{:S(2)}, u32[]{:S(2)}) %collective-permute-start.3) | collective-permute-done | bytes 24608 | tf_op jit(solution)/shard_map/ppermute | solution.py:155
  114.1 16.9 %collective-permute-done.18 = bf16[2,1024,256]{1,2,0:T(8,128)(2,1)} collective-permute-done((bf16[2,1024,256]{1,2,0:T(8,128)(2,1)}, bf16[2,1024,256]{1,2,0:T(8,128)(2,1)}, u32[]{:S(2)}, u32[]{:S(2)}) %collective-permute-start.18) | collective-permute-done | bytes 1048608 | tf_op jit(solution)/shard_map/ppermute | solution.py:155
  137.2 6.3 collective-permute-done.8
  145.2 10.0 %add_convert_fusion.x_ref = bf16[1024,3072]{1,0:T(8,128)(2,1)S(1)} fusion(f32[3072]{0:T(1024)S(1)} %add.258, bf16[512,1536]{1,0:T(8,128)(2,1)} %collective-permute-done.6, bf16[512,1536]{1,0:T(8,128)(2,1)} %collective-permute-done.5, bf16[512,1536]{1,0:T(8,128)(2,1)} %collective-permute-done.4, bf16[512,1536]{1,0:T(8,128)(2,1)} %param.17, ...), kind=kOutput, calls=%fused_computation.12 | convolution fusion | flops 6483345408 | bytes 14708736 | tf_op jit(solution)/shard_map/dot_general | solution.py:308
  155.3 31.8 %attend.1 = (bf16[1024,1024]{1,0:T(8,128)(2,1)S(1)}, f32[8,2,1024]{2,1,0:T(2,128)S(1)}) custom-call(f32[16]{0:T(128)S(1)} %fusion.46.slopes, bf16[1024,3072]{1,0:T(8,128)(2,1)S(1)} %add_convert_fusion.x_ref), custom_call_target="tpu_custom_call" | custom-call | flops 17179869184 | bytes 8388608 | tf_op jit(solution)/shard_map/attend/pallas_call | solution.py:72
  191.9 6.8 fusion.66
  201.3 19.6 %fusion.29 = f32[1024,4096]{1,0:T(8,128)} fusion(bf16[512,2048]{1,0:T(8,128)(2,1)} %collective-permute-done.12, bf16[512,2048]{1,0:T(8,128)(2,1)} %collective-permute-done.11, bf16[512,2048]{1,0:T(8,128)(2,1)} %collective-permute-done.10, bf16[512,2048]{1,0:T(8,128)(2,1)} %param.23, f32[1024,1024]{0,1:T(8,128)} %copy-done.5, f32[1024]{0:T(1024)S(1)} %bitcast.140, ...), kind=kOutput, calls=%fused_computation.84 | convolution fusion | flops 8628731904 | bytes 29376512 | tf_op jit(solution)/shard_map/dot_general | solution.py:312
  220.9 27.3 %convert_reduce_fusion = (f32[4096]{0:T(1024)S(1)}, bf16[1024,4096]{1,0:T(8,128)(2,1)}) fusion(f32[1024,4096]{1,0:T(8,128)} %fusion.29, f32[4096]{0:T(1024)S(1)} %bitcast.124, bf16[2048,512]{1,0:T(8,128)(2,1)} %collective-permute-done.15, bf16[2048,512]{1,0:T(8,128)(2,1)} %collective-permute-done.14, bf16[2048,512]{1,0:T(8,128)(2,1)} %collective-permute-done.13, ...), kind=kOutput, calls=%fused_computation.9 | convolution fusion | flops 8724148224 | bytes 35684352 | tf_op jit(solution)/shard_map/dot_general | solution.py:24
  248.2 19.8 %multiply_reduce_fusion = (f32[1024]{0:T(1024)S(1)}, f32[1024]{0:T(1024)S(1)}, f32[1024]{0:T(1024)S(1)}, f32[1024]{0:T(1024)S(1)}, f32[1024,1024]{0,1:T(8,128)}) fusion(f32[1024,1024]{0,1:T(8,128)} %copy-done.5, f32[1024]{0:T(1024)S(1)} %add_rsqrt_fusion, f32[1024]{0:T(1024)S(1)} %broadcast_multiply_fusion.4, f32[1024]{0:T(1024)S(1)} %bitcast.117, ...), kind=kOutput, calls=%fused_computation.47 | convolution fusion | flops 8632922112 | bytes 25194496 | tf_op jit(solution)/shard_map/dot_general | solution.py:24
  268.0 5.6 fusion.59
  281.1 49.7 %attend_back.1 = bf16[1024,3072]{1,0:T(8,128)(2,1)S(1)} custom-call(f32[16]{0:T(128)S(1)} %fusion.46.slopes, bf16[1024,3072]{1,0:T(8,128)(2,1)} %copy-done.1, bf16[1024,1024]{1,0:T(8,128)(2,1)S(1)} %convolution_convert_fusion.4.do_ref, f32[8,2,1024]{2,1,0:T(2,128)S(1)} %get-tuple-element.17.lse_ref), custom_call_target="tpu_custom_call" | custom-call | flops 42949672960 | bytes 16777216 | tf_op jit(solution)/shard_map/attend_back/pallas_call | solution.py:132
  335.1 17.0 %fusion.20 = (f32[1024]{0:T(1024)S(1)}, f32[1024]{0:T(1024)S(1)}, f32[1024]{0:T(1024)S(1)}, f32[1024]{0:T(1024)S(1)}, f32[1024,1024]{0,1:T(8,128)}) fusion(f32[1024]{0:T(1024)S(1)} %copy-done.32, f32[1024]{0:T(1024)S(1)} %copy-done.24, bf16[1024,512]{0,1:T(8,128)(2,1)S(1)} %copy-done.11, bf16[1024,512]{0,1:T(8,128)(2,1)S(1)} %copy-done.8, ...), kind=kOutput, calls=%fused_computation.40 | convolution fusion | flops 6481244160 | bytes 18903040 | tf_op jit(solution)/shard_map/dot_general | solution.py:24
  353.1 21.9 %add_convert_fusion.1 = bf16[1024,1024]{0,1:T(8,128)(2,1)S(1)} fusion(f32[1024,1024]{0,1:T(8,128)} %copy-done.5, f32[1024]{0:T(1024)S(1)} %bitcast.144, bf16[2048,512]{1,0:T(8,128)(2,1)} %collective-permute-done.15, bf16[2048,512]{1,0:T(8,128)(2,1)} %collective-permute-done.14, bf16[2048,512]{1,0:T(8,128)(2,1)} %collective-permute-done.13, ...), kind=kOutput, calls=%fused_computation.49 | convolution fusion | flops 8668577792 | bytes 31477760 | tf_op jit(solution)/shard_map/dot_general | solution.py:314
  375.1 4.9 fusion.19
  389.0 11.0 %convolution_convert_fusion.2 = bf16[1024,3072]{1,0:T(8,128)(2,1)S(1)} fusion(bf16[1024,3072]{1,0:T(8,128)(2,1)} %copy-done, f32[1024]{0:T(1024)S(1)} %bitcast.143, f32[1024]{0:T(1024)S(1)} %bitcast.123, f32[1024]{0:T(1024)S(1)} %copy-done.32, f32[1024]{0:T(1024)S(1)} %copy-done.24, bf16[1024,512]{0,1:T(8,128)(2,1)S(1)} %copy-done.11, ...), kind=kOutput, calls=%fused_computation.24 | convolution fusion | flops 6455033856 | bytes 14696448 | tf_op jit(solution)/shard_map/dot_general | solution.py:24
  405.8 19.6 %convolution_convert_fusion = bf16[4096,1024]{1,0:T(8,128)(2,1)} fusion(bf16[1024,512]{0,1:T(8,128)(2,1)} %collective-permute-done.19, bf16[1024,512]{0,1:T(8,128)(2,1)S(1)} %copy-done.18, f32[1024,4096]{1,0:T(8,128)} %fusion.29, f32[4096]{0:T(1024)S(1)} %bitcast.126), kind=kOutput, calls=%fused_computation.17 | convolution fusion | flops 8640266240 | bytes 27279360 | tf_op jit(solution)/shard_map/dot_general | solution.py:24
  429.9 14.9 %convolution_convert_fusion.1 = bf16[1024,4096]{1,0:T(8,128)(2,1)} fusion(bf16[1024,4096]{1,0:T(8,128)(2,1)} %get-tuple-element.70, f32[1024,1024]{0,1:T(8,128)S(1)} %copy-done.6, f32[1024]{0:T(1024)S(1)} %bitcast.141, f32[1024]{0:T(1024)S(1)} %bitcast.119, f32[1024]{0:T(1024)S(1)} %copy-done.34, f32[1024]{0:T(1024)S(1)} %copy-done.26), kind=kOutput, calls=%fused_computation.18 | convolution fusion | flops 8599371776 | bytes 20987904 | tf_op jit(solution)/shard_map/dot_general | solution.py:24
  447.0 5.0 slice.336
  476.3 4.5 collective-permute-done.39
  481.8 23.4 %collective-permute-done.28 = bf16[512,1536]{1,0:T(8,128)(2,1)} collective-permute-done((bf16[512,1536]{1,0:T(8,128)(2,1)}, bf16[512,1536]{1,0:T(8,128)(2,1)}, u32[]{:S(2)}, u32[]{:S(2)}) %collective-permute-start.28) | collective-permute-done | bytes 1572896 | tf_op jit(solution)/shard_map/ppermute | solution.py:155
  517.4 9.1 %collective-permute-done.29 = bf16[256,1536]{1,0:T(8,128)(2,1)} collective-permute-done((bf16[256,1536]{1,0:T(8,128)(2,1)}, bf16[256,1536]{1,0:T(8,128)(2,1)}, u32[]{:S(2)}, u32[]{:S(2)}) %collective-permute-start.29) | collective-permute-done | bytes 786464 | tf_op jit(solution)/shard_map/ppermute | solution.py:218
  529.4 4.7 convert_add_fusion
  539.1 33.4 %collective-permute-done.44 = bf16[512,2048]{1,0:T(8,128)(2,1)S(1)} collective-permute-done((bf16[512,2048]{1,0:T(8,128)(2,1)}, bf16[512,2048]{1,0:T(8,128)(2,1)S(1)}, u32[]{:S(2)}, u32[]{:S(2)}) %collective-permute-start.44) | collective-permute-done | bytes 2097184 | tf_op jit(solution)/shard_map/ppermute | solution.py:155
  575.5 40.8 %collective-permute-done.52 = bf16[2048,512]{1,0:T(8,128)(2,1)S(1)} collective-permute-done((bf16[2048,512]{1,0:T(8,128)(2,1)S(1)}, bf16[2048,512]{1,0:T(8,128)(2,1)S(1)}, u32[]{:S(2)}, u32[]{:S(2)}) %collective-permute-start.52) | collective-permute-done | bytes 2097184 | tf_op jit(solution)/shard_map/ppermute | solution.py:155
  620.0 21.1 %collective-permute-done.53 = bf16[1024,512]{1,0:T(8,128)(2,1)S(1)} collective-permute-done((bf16[1024,512]{1,0:T(8,128)(2,1)S(1)}, bf16[1024,512]{1,0:T(8,128)(2,1)S(1)}, u32[]{:S(2)}, u32[]{:S(2)}) %collective-permute-start.53) | collective-permute-done | bytes 1048608 | tf_op jit(solution)/shard_map/ppermute | solution.py:218
  643.3 16.0 %collective-permute-done.54 = bf16[512,512]{1,0:T(8,128)(2,1)S(1)} collective-permute-done((bf16[512,512]{1,0:T(8,128)(2,1)S(1)}, bf16[512,512]{1,0:T(8,128)(2,1)S(1)}, u32[]{:S(2)}, u32[]{:S(2)}) %collective-permute-start.54) | collective-permute-done | bytes 524320 | tf_op jit(solution)/shard_map/ppermute | solution.py:218
  662.9 14.6 %collective-permute-done.55 = bf16[256,512]{1,0:T(8,128)(2,1)S(1)} collective-permute-done((bf16[256,512]{1,0:T(8,128)(2,1)S(1)}, bf16[256,512]{1,0:T(8,128)(2,1)S(1)}, u32[]{:S(2)}, u32[]{:S(2)}) %collective-permute-start.55) | collective-permute-done | bytes 262176 | tf_op jit(solution)/shard_map/ppermute | solution.py:218
  677.7 11.0 %collective-permute-done.48 = bf16[64,2048]{1,0:T(8,128)(2,1)S(1)} collective-permute-done((bf16[64,2048]{1,0:T(8,128)(2,1)S(1)}, bf16[64,2048]{1,0:T(8,128)(2,1)S(1)}, u32[]{:S(2)}, u32[]{:S(2)}) %collective-permute-start.48) | collective-permute-done | bytes 262176 | tf_op jit(solution)/shard_map/ppermute | solution.py:224
  696.9 8.7 %collective-permute-done.49 = bf16[128,2048]{1,0:T(8,128)(2,1)S(1)} collective-permute-done((bf16[128,2048]{1,0:T(8,128)(2,1)S(1)}, bf16[128,2048]{1,0:T(8,128)(2,1)S(1)}, u32[]{:S(2)}, u32[]{:S(2)}) %collective-permute-start.49) | collective-permute-done | bytes 524320 | tf_op jit(solution)/shard_map/ppermute | solution.py:224
  709.9 9.7 %collective-permute-done.57 = bf16[512,512]{1,0:T(8,128)(2,1)S(1)} collective-permute-done((bf16[512,512]{1,0:T(8,128)(2,1)S(1)}, bf16[512,512]{1,0:T(8,128)(2,1)S(1)}, u32[]{:S(2)}, u32[]{:S(2)}) %collective-permute-start.57) | collective-permute-done | bytes 524320 | tf_op jit(solution)/shard_map/ppermute | solution.py:224
  728.4 25.8 %collective-permute-done.42 = bf16[256,512]{1,0:T(8,128)(2,1)S(1)} collective-permute-done((bf16[256,512]{1,0:T(8,128)(2,1)S(1)}, bf16[256,512]{1,0:T(8,128)(2,1)S(1)}, u32[]{:S(2)}, u32[]{:S(2)}) %collective-permute-start.42) | collective-permute-done | bytes 262176 | tf_op jit(solution)/shard_map/ppermute | solution.py:224
  760.5 15.0 %collective-permute-done.58 = bf16[1024,512]{1,0:T(8,128)(2,1)S(1)} collective-permute-done((bf16[1024,512]{1,0:T(8,128)(2,1)S(1)}, bf16[1024,512]{1,0:T(8,128)(2,1)S(1)}, u32[]{:S(2)}, u32[]{:S(2)}) %collective-permute-start.58) | collective-permute-done | bytes 1048608 | tf_op jit(solution)/shard_map/ppermute | solution.py:224
  (344 shorter events, 166.4 us)
Async XLA Ops:
  0.6 111.5 %collective-permute-start.4 = (bf16[512,1536]{1,0:T(8,128)(2,1)}, bf16[512,1536]{1,0:T(8,128)(2,1)}, u32[]{:S(2)}, u32[]{:S(2)}) collective-permute-start(bf16[512,1536]{1,0:T(8,128)(2,1)} %param.17), channel_id=1, source_target_pairs={{0,1},{1,0},{2,3},{3,2},{4,5},{5,4},{6,7},{7,6},{8,9},{9,8},{10,11... | collective-permute-start | bytes 4718600 | tf_op jit(solution)/shard_map/ppermute | solution.py:155
  3.6 139.9 %collective-permute-start.5 = (bf16[512,1536]{1,0:T(8,128)(2,1)}, bf16[512,1536]{1,0:T(8,128)(2,1)}, u32[]{:S(2)}, u32[]{:S(2)}) collective-permute-start(bf16[512,1536]{1,0:T(8,128)(2,1)} %param.17), channel_id=1, source_target_pairs={{0,2},{2,0},{1,3},{3,1},{4,6},{6,4},{5,7},{7,5},{8,10},{10,8},{9,1... | collective-permute-start | bytes 4718600 | tf_op jit(solution)/shard_map/ppermute | solution.py:155
  12.6 95.7 %collective-permute-start = (bf16[2,1024,256]{1,2,0:T(8,128)(2,1)}, bf16[2,1024,256]{1,2,0:T(8,128)(2,1)}, u32[]{:S(2)}, u32[]{:S(2)}) collective-permute-start(bf16[2,1024,256]{1,2,0:T(8,128)(2,1)} %bitcast.1), channel_id=1, source_target_pairs={{0,1},{1,0},{2,3},{3,2},{4,5},{5,4},{6,7},{7,6},{8,9},{9,8},{10,11... | collective-permute-start | bytes 3145736 | tf_op jit(solution)/shard_map/ppermute | solution.py:155
  12.7 132.0 %collective-permute-start.10 = (bf16[512,2048]{1,0:T(8,128)(2,1)}, bf16[512,2048]{1,0:T(8,128)(2,1)}, u32[]{:S(2)}, u32[]{:S(2)}) collective-permute-start(bf16[512,2048]{1,0:T(8,128)(2,1)} %param.23), channel_id=1, source_target_pairs={{0,1},{1,0},{2,3},{3,2},{4,5},{5,4},{6,7},{7,6},{8,9},{9,8},{10,11... | collective-permute-start | bytes 6291464 | tf_op jit(solution)/shard_map/ppermute | solution.py:155
  17.4 88.8 %collective-permute-start.3 = (f32[2,3072]{1,0:T(2,128)S(1)}, f32[2,3072]{1,0:T(2,128)S(1)}, u32[]{:S(2)}, u32[]{:S(2)}) collective-permute-start(f32[2,3072]{1,0:T(2,128)S(1)} %get-tuple-element.55), channel_id=1, source_target_pairs={{0,1},{1,0},{2,3},{3,2},{4,5},{5,4},{6,7},{7,6},{8,9},{9,8},{10,11... | collective-permute-start | bytes 73736 | tf_op jit(solution)/shard_map/ppermute | solution.py:155
  112.1 32.8 %collective-permute-start.6 = (bf16[512,1536]{1,0:T(8,128)(2,1)}, bf16[512,1536]{1,0:T(8,128)(2,1)}, u32[]{:S(2)}, u32[]{:S(2)}) collective-permute-start(bf16[512,1536]{1,0:T(8,128)(2,1)} %collective-permute-done.4), channel_id=1, source_target_pairs={{0,2},{2,0},{1,3},{3,1},{4,6},{6,4},{5,7},{7,5},{8,10},{10,8},{9,1... | collective-permute-start | bytes 4718600 | tf_op jit(solution)/shard_map/ppermute | solution.py:155
  136.1 50.9 %collective-permute-start.7 = (bf16[512,512]{1,0:T(8,128)(2,1)S(1)}, bf16[512,512]{1,0:T(8,128)(2,1)}, u32[]{:S(2)}, u32[]{:S(2)}) collective-permute-start(bf16[512,512]{1,0:T(8,128)(2,1)S(1)} %copy-done.41), channel_id=1, source_target_pairs={{0,2},{2,0},{1,3},{3,1},{4,6},{6,4},{5,7},{7,5},{8,10},{10,8},{9,1... | collective-permute-start | bytes 1572872 | tf_op jit(solution)/shard_map/ppermute | solution.py:155
  143.6 57.7 %collective-permute-start.11 = (bf16[512,2048]{1,0:T(8,128)(2,1)}, bf16[512,2048]{1,0:T(8,128)(2,1)}, u32[]{:S(2)}, u32[]{:S(2)}) collective-permute-start(bf16[512,2048]{1,0:T(8,128)(2,1)} %param.23), channel_id=1, source_target_pairs={{0,2},{2,0},{1,3},{3,1},{4,6},{6,4},{5,7},{7,5},{8,10},{10,8},{9,1... | collective-permute-start | bytes 6291464 | tf_op jit(solution)/shard_map/ppermute | solution.py:155
  143.6 48.4 %collective-permute-start.14 = (bf16[2048,512]{1,0:T(8,128)(2,1)}, bf16[2048,512]{1,0:T(8,128)(2,1)}, u32[]{:S(2)}, u32[]{:S(2)}) collective-permute-start(bf16[2048,512]{1,0:T(8,128)(2,1)} %param.25), channel_id=1, source_target_pairs={{0,1},{1,0},{2,3},{3,2},{4,5},{5,4},{6,7},{7,6},{8,9},{9,8},{10,11... | collective-permute-start | bytes 6291464 | tf_op jit(solution)/shard_map/ppermute | solution.py:155
  144.7 42.6 %collective-permute-start.9 = (bf16[512,512]{1,0:T(8,128)(2,1)}, bf16[512,512]{1,0:T(8,128)(2,1)}, u32[]{:S(2)}, u32[]{:S(2)}) collective-permute-start(bf16[512,512]{1,0:T(8,128)(2,1)} %collective-permute-done.8), channel_id=1, source_target_pairs={{0,2},{2,0},{1,3},{3,1},{4,6},{6,4},{5,7},{7,5},{8,10},{10,8},{9,1... | collective-permute-start | bytes 1572872 | tf_op jit(solution)/shard_map/ppermute | solution.py:155
  144.9 56.3 %collective-permute-start.12 = (bf16[512,2048]{1,0:T(8,128)(2,1)}, bf16[512,2048]{1,0:T(8,128)(2,1)}, u32[]{:S(2)}, u32[]{:S(2)}) collective-permute-start(bf16[512,2048]{1,0:T(8,128)(2,1)} %collective-permute-done.10), channel_id=1, source_target_pairs={{0,2},{2,0},{1,3},{3,1},{4,6},{6,4},{5,7},{7,5},{8,10},{10,8},{9,1... | collective-permute-start | bytes 6291464 | tf_op jit(solution)/shard_map/ppermute | solution.py:155
  187.0 33.8 %collective-permute-start.13 = (bf16[2048,512]{1,0:T(8,128)(2,1)}, bf16[2048,512]{1,0:T(8,128)(2,1)}, u32[]{:S(2)}, u32[]{:S(2)}) collective-permute-start(bf16[2048,512]{1,0:T(8,128)(2,1)} %param.25), channel_id=1, source_target_pairs={{0,2},{2,0},{1,3},{3,1},{4,6},{6,4},{5,7},{7,5},{8,10},{10,8},{9,1... | collective-permute-start | bytes 6291464 | tf_op jit(solution)/shard_map/ppermute | solution.py:155
  187.3 33.5 %collective-permute-start.19 = (bf16[1024,512]{0,1:T(8,128)(2,1)}, bf16[1024,512]{0,1:T(8,128)(2,1)}, u32[]{:S(2)}, u32[]{:S(2)}) collective-permute-start(bf16[1024,512]{0,1:T(8,128)(2,1)} %get-tuple-element.34), channel_id=1, source_target_pairs={{0,2},{2,0},{1,3},{3,1},{4,6},{6,4},{5,7},{7,5},{8,10},{10,8},{9,1... | collective-permute-start | bytes 3145736 | tf_op jit(solution)/shard_map/ppermute | solution.py:155
  382.9 74.6 %collective-permute-start.16 = (bf16[1024,512]{0,1:T(8,128)(2,1)}, bf16[1024,512]{0,1:T(8,128)(2,1)}, u32[]{:S(2)}, u32[]{:S(2)}) collective-permute-start(bf16[1024,512]{0,1:T(8,128)(2,1)} %get-tuple-element.39), channel_id=1, source_target_pairs={{0,2},{2,0},{1,3},{3,1},{4,6},{6,4},{5,7},{7,5},{8,10},{10,8},{9,1... | collective-permute-start | bytes 3145736 | tf_op jit(solution)/shard_map/ppermute | solution.py:155
  387.2 85.0 %collective-permute-start.20 = (bf16[1024,512]{0,1:T(8,128)(2,1)}, bf16[1024,512]{0,1:T(8,128)(2,1)}, u32[]{:S(2)}, u32[]{:S(2)}) collective-permute-start(bf16[1024,512]{0,1:T(8,128)(2,1)} %get-tuple-element.31), channel_id=1, source_target_pairs={{0,2},{2,0},{1,3},{3,1},{4,6},{6,4},{5,7},{7,5},{8,10},{10,8},{9,1... | collective-permute-start | bytes 3145736 | tf_op jit(solution)/shard_map/ppermute | solution.py:155
  401.8 60.3 %collective-permute-start.27 = (bf16[512,3072]{1,0:T(8,128)(2,1)}, bf16[512,3072]{1,0:T(8,128)(2,1)}, u32[]{:S(2)}, u32[]{:S(2)}) collective-permute-start(bf16[512,3072]{1,0:T(8,128)(2,1)} %slice.312), channel_id=1, source_target_pairs={{0,2},{2,0},{1,3},{3,1},{4,6},{6,4},{5,7},{7,5},{8,10},{10,8},{9,1... | collective-permute-start | bytes 9437192 | tf_op jit(solution)/shard_map/ppermute | solution.py:155
  455.7 54.9 %collective-permute-start.43 = (bf16[512,4096]{1,0:T(8,128)(2,1)}, bf16[512,4096]{1,0:T(8,128)(2,1)}, u32[]{:S(2)}, u32[]{:S(2)}) collective-permute-start(bf16[512,4096]{1,0:T(8,128)(2,1)} %slice.336), channel_id=1, source_target_pairs={{0,2},{2,0},{1,3},{3,1},{4,6},{6,4},{5,7},{7,5},{8,10},{10,8},{9,1... | collective-permute-start | bytes 12582920 | tf_op jit(solution)/shard_map/ppermute | solution.py:155
  457.5 71.9 %collective-permute-start.51 = (bf16[4096,512]{1,0:T(8,128)(2,1)}, bf16[4096,512]{1,0:T(8,128)(2,1)}, u32[]{:S(2)}, u32[]{:S(2)}) collective-permute-start(bf16[4096,512]{1,0:T(8,128)(2,1)} %slice.347), channel_id=1, source_target_pairs={{0,2},{2,0},{1,3},{3,1},{4,6},{6,4},{5,7},{7,5},{8,10},{10,8},{9,1... | collective-permute-start | bytes 12582920 | tf_op jit(solution)/shard_map/ppermute | solution.py:155
  467.7 37.6 %collective-permute-start.28 = (bf16[512,1536]{1,0:T(8,128)(2,1)}, bf16[512,1536]{1,0:T(8,128)(2,1)}, u32[]{:S(2)}, u32[]{:S(2)}) collective-permute-start(bf16[512,1536]{1,0:T(8,128)(2,1)} %slice.454), channel_id=1, source_target_pairs={{0,1},{1,0},{2,3},{3,2},{4,5},{5,4},{6,7},{7,6},{8,9},{9,8},{10,11... | collective-permute-start | bytes 4718600 | tf_op jit(solution)/shard_map/ppermute | solution.py:155
  472.2 249.2 %collective-permute-start.17 = (bf16[2,1024,256]{2,1,0:T(8,128)(2,1)}, bf16[2,1024,256]{2,1,0:T(8,128)(2,1)}, u32[]{:S(2)}, u32[]{:S(2)}) collective-permute-start(bf16[2,1024,256]{2,1,0:T(8,128)(2,1)} %get-tuple-element.37), channel_id=1, source_target_pairs={{0,1},{1,0},{2,3},{3,2},{4,5},{5,4},{6,7},{7,6},{8,9},{9,8},{10,11... | collective-permute-start | bytes 3145736 | tf_op jit(solution)/shard_map/ppermute | solution.py:155
  481.4 207.8 %collective-permute-start.40 = (bf16[64,512]{1,0:T(8,128)(2,1)}, bf16[64,512]{1,0:T(8,128)(2,1)}, u32[]{:S(2)}, u32[]{:S(2)}) collective-permute-start(bf16[64,512]{1,0:T(8,128)(2,1)} %add_convert_fusion.6), channel_id=1, source_target_pairs={{0,16},{4,20},{8,24},{12,28},{16,0},{20,4},{24,8},{28,12},{1,17},{... | collective-permute-start | bytes 196616 | tf_op jit(solution)/shard_map/ppermute | solution.py:224
  515.9 56.6 %collective-permute-start.44 = (bf16[512,2048]{1,0:T(8,128)(2,1)}, bf16[512,2048]{1,0:T(8,128)(2,1)S(1)}, u32[]{:S(2)}, u32[]{:S(2)}) collective-permute-start(bf16[512,2048]{1,0:T(8,128)(2,1)} %slice.453), channel_id=1, source_target_pairs={{0,1},{1,0},{2,3},{3,2},{4,5},{5,4},{6,7},{7,6},{8,9},{9,8},{10,11... | collective-permute-start | bytes 6291464 | tf_op jit(solution)/shard_map/ppermute | solution.py:155
  534.4 81.9 %collective-permute-start.52 = (bf16[2048,512]{1,0:T(8,128)(2,1)S(1)}, bf16[2048,512]{1,0:T(8,128)(2,1)S(1)}, u32[]{:S(2)}, u32[]{:S(2)}) collective-permute-start(bf16[2048,512]{1,0:T(8,128)(2,1)S(1)} %slice.452), channel_id=1, source_target_pairs={{0,1},{1,0},{2,3},{3,2},{4,5},{5,4},{6,7},{7,6},{8,9},{9,8},{10,11... | collective-permute-start | bytes 6291464 | tf_op jit(solution)/shard_map/ppermute | solution.py:155
  538.1 36.8 %collective-permute-start.31 = (bf16[64,1536]{1,0:T(8,128)(2,1)S(1)}, bf16[64,1536]{1,0:T(8,128)(2,1)S(1)}, u32[]{:S(2)}, u32[]{:S(2)}) collective-permute-start(bf16[64,1536]{1,0:T(8,128)(2,1)S(1)} %select_convert_fusion.9), channel_id=1, source_target_pairs={{0,16},{4,20},{8,24},{12,28},{16,0},{20,4},{24,8},{28,12},{1,17},{... | collective-permute-start | bytes 589832 | tf_op jit(solution)/shard_map/ppermute | solution.py:218
  573.3 45.4 %collective-permute-start.45 = (bf16[256,2048]{1,0:T(8,128)(2,1)S(1)}, bf16[256,2048]{1,0:T(8,128)(2,1)S(1)}, u32[]{:S(2)}, u32[]{:S(2)}) collective-permute-start(bf16[256,2048]{1,0:T(8,128)(2,1)S(1)} %select_convert_fusion.1), channel_id=1, source_target_pairs={{0,4},{4,0},{8,12},{12,8},{16,20},{20,16},{24,28},{28,24},{1,5},{5... | collective-permute-start | bytes 3145736 | tf_op jit(solution)/shard_map/ppermute | solution.py:218
  575.0 87.8 %collective-permute-start.32 = (bf16[64,1536]{1,0:T(8,128)(2,1)S(1)}, bf16[64,1536]{1,0:T(8,128)(2,1)S(1)}, u32[]{:S(2)}, u32[]{:S(2)}) collective-permute-start(bf16[64,1536]{1,0:T(8,128)(2,1)S(1)} %add_convert_fusion.5), channel_id=1, source_target_pairs={{0,16},{4,20},{8,24},{12,28},{16,0},{20,4},{24,8},{28,12},{1,17},{... | collective-permute-start | bytes 589832 | tf_op jit(solution)/shard_map/ppermute | solution.py:224
  662.9 31.7 %collective-permute-start.33 = (bf16[128,1536]{1,0:T(8,128)(2,1)S(1)}, bf16[128,1536]{1,0:T(8,128)(2,1)S(1)}, u32[]{:S(2)}, u32[]{:S(2)}) collective-permute-start(bf16[128,1536]{1,0:T(8,128)(2,1)S(1)} %maximum_select_fusion.15), channel_id=1, source_target_pairs={{0,8},{4,12},{8,0},{12,4},{16,24},{20,28},{24,16},{28,20},{1,9},{5... | collective-permute-start | bytes 1179656 | tf_op jit(solution)/shard_map/ppermute | solution.py:224
  689.1 36.6 %collective-permute-start.21 = (bf16[2,1024,256]{2,1,0:T(8,128)(2,1)S(1)}, bf16[2,1024,256]{2,1,0:T(8,128)(2,1)S(1)}, u32[]{:S(2)}, u32[]{:S(2)}) collective-permute-start(bf16[2,1024,256]{2,1,0:T(8,128)(2,1)S(1)} %get-tuple-element.29), channel_id=1, source_target_pairs={{0,1},{1,0},{2,3},{3,2},{4,5},{5,4},{6,7},{7,6},{8,9},{9,8},{10,11... | collective-permute-start | bytes 3145736 | tf_op jit(solution)/shard_map/ppermute | solution.py:155
  705.6 49.7 %collective-permute-start.34 = (bf16[256,1536]{1,0:T(8,128)(2,1)S(1)}, bf16[256,1536]{1,0:T(8,128)(2,1)S(1)}, u32[]{:S(2)}, u32[]{:S(2)}) collective-permute-start(bf16[256,1536]{1,0:T(8,128)(2,1)S(1)} %maximum_select_fusion.11), channel_id=1, source_target_pairs={{0,4},{4,0},{8,12},{12,8},{16,20},{20,16},{24,28},{28,24},{1,5},{5... | collective-permute-start | bytes 2359304 | tf_op jit(solution)/shard_map/ppermute | solution.py:224
  708.4 49.2 %collective-permute-start.50 = (bf16[256,2048]{1,0:T(8,128)(2,1)S(1)}, bf16[256,2048]{1,0:T(8,128)(2,1)S(1)}, u32[]{:S(2)}, u32[]{:S(2)}) collective-permute-start(bf16[256,2048]{1,0:T(8,128)(2,1)S(1)} %maximum_select_fusion.9), channel_id=1, source_target_pairs={{0,4},{4,0},{8,12},{12,8},{16,20},{20,16},{24,28},{28,24},{1,5},{5... | collective-permute-start | bytes 3145736 | tf_op jit(solution)/shard_map/ppermute | solution.py:224
  719.6 34.6 %collective-permute-start.42 = (bf16[256,512]{1,0:T(8,128)(2,1)S(1)}, bf16[256,512]{1,0:T(8,128)(2,1)S(1)}, u32[]{:S(2)}, u32[]{:S(2)}) collective-permute-start(bf16[256,512]{1,0:T(8,128)(2,1)S(1)} %maximum_select_fusion.16), channel_id=1, source_target_pairs={{0,4},{4,0},{8,12},{12,8},{16,20},{20,16},{24,28},{28,24},{1,5},{5... | collective-permute-start | bytes 786440 | tf_op jit(solution)/shard_map/ppermute | solution.py:224
  721.4 54.1 %collective-permute-start.58 = (bf16[1024,512]{1,0:T(8,128)(2,1)S(1)}, bf16[1024,512]{1,0:T(8,128)(2,1)S(1)}, u32[]{:S(2)}, u32[]{:S(2)}) collective-permute-start(bf16[1024,512]{1,0:T(8,128)(2,1)S(1)} %maximum_select_fusion.10), channel_id=1, source_target_pairs={{0,4},{4,0},{8,12},{12,8},{16,20},{20,16},{24,28},{28,24},{1,5},{5... | collective-permute-start | bytes 3145736 | tf_op jit(solution)/shard_map/ppermute | solution.py:224
  (72 other events, 1612.2 us)
